TPU v7x, 32 devices: a whole 2x2x4 slice. The times are simulated.
32 devices in a mesh: parts: 2 (over x), gx: 4 (over y, core), gy: 4 (over z).
Axes of the slice: x: 2, y: 2, z: 4, core: 2. Of those that a mesh axis runs over, the one named last changes fastest.
Arguments:
- forcing_right_side: float32 [32, 32, 1024], P(('parts', 'gx'), 'gy'), parts along dimension 0, may hold values from -18 to 18
- earlier_warmth: float32 [32, 32, 1024], P(('parts', 'gx'), 'gy'), parts along dimension 0, may hold values from 0 to 2
- matter_condition: int32 [32, 32, 1024], P(('parts', 'gx'), 'gy'), parts along dimension 0, may hold values from 0 to 2
- compressed_slot_number: int32 [32, 32, 1024], P(('parts', 'gx'), 'gy'), parts along dimension 0, may hold values from 0 to 127
- normal_draw_factor: float32 [32, 32, 1024], P(('parts', 'gx'), 'gy'), parts along dimension 0, may hold values from -6 to 6
Outputs:
- solution: float32 [32, 32, 1024], P(('parts', 'gx'), 'gy'), parts along dimension 0
- residual: float32 [32, 32, 1024], P(('parts', 'gx'), 'gy'), parts along dimension 0
There are 2 independent parts, one for each index of `parts`. A program takes and returns all parts, laid end to end along the dimension named above; each array names one. Nothing has to cross between parts.
Inputs may be any that keep to these rules, and one draw needn't show every extreme that they name: `matter_condition`: phase labels the cell as powder, solid or liquid. `compressed_slot_number`: each cell's row of the sketch.
All inputs are finite; a program needn't handle non-finite values.
Results may differ from a plain program's by a relative error of at most 0.0003.
Values sent between devices are 32-bit elements; how exact they have to be, the bound alone decides.
A program may use at most 64 MiB of HBM per device.

v0:
```python
import math

import jax
import jax.numpy as jnp
from jax import lax
from jax.sharding import PartitionSpec as P

BASIS = 2
SKETCH = 128


epsilon = 1e-06
highest = lax.Precision.HIGHEST


def padded_2(block, sides, width):
    for axis, dim in sides:
        count = lax.axis_size(axis)
        forward = [(i, i + 1) for i in range(count - 1)]
        backward = [(target, source) for source, target in forward]
        low = lax.ppermute(
            lax.slice_in_dim(block, block.shape[dim] - width, None, axis=dim), axis, forward
        )
        high = lax.ppermute(lax.slice_in_dim(block, 0, width, axis=dim), axis, backward)
        block = jnp.concatenate([low, block, high], axis=dim)
    return block


def medium_traits(earlier_warmth, matter_condition):
    datum_offset = jnp.where(
        matter_condition == 0, 0.2, jnp.where(matter_condition == 1, 1.0, 0.6)
    ).astype(jnp.float32)
    spreading_rate = datum_offset * (0.5 + earlier_warmth)
    volumetric_retention = jnp.where(
        matter_condition == 0, 1.0, jnp.where(matter_condition == 1, 2.0, 1.5)
    ).astype(jnp.float32)
    return (spreading_rate, volumetric_retention)


def harmonic(first, second):
    return 2.0 * first * second / (first + second)


def beside_all(padded, field):
    depth = jnp.pad(field, ((0, 0), (0, 0), (1, 1)))
    return [
        padded[2:, 1:-1],
        padded[:-2, 1:-1],
        padded[1:-1, 2:],
        padded[1:-1, :-2],
        depth[:, :, 2:],
        depth[:, :, :-2],
    ]


def sketch_local(field, compressed_slot_number, normal_draw_factor):
    weighted = (normal_draw_factor * field).reshape(-1)
    row_ids = compressed_slot_number.reshape(-1)
    cells = weighted.shape[0]
    block_size = math.gcd(cells, 8192)
    block_count = cells // block_size
    weighted = weighted.reshape(block_count, block_size)
    row_ids = row_ids.reshape(block_count, block_size)
    slots = lax.broadcasted_iota(jnp.int32, (1, SKETCH), 1)

    def add_block(totals, block_pair):
        block_vals, block_rows = block_pair
        onehot = (block_rows[:, None] == slots).astype(jnp.float32)
        return (totals + jnp.dot(block_vals, onehot, precision=highest), None)

    totals, unused = lax.scan(add_block, jnp.zeros((SKETCH,), jnp.float32), (weighted, row_ids))
    return totals


def solve_small(hess, scale_norm):
    width_count = hess.shape[1]
    gram_matrix = jnp.dot(hess.T, hess, precision=highest)
    target = scale_norm * hess[0]
    factor = jnp.linalg.cholesky(gram_matrix)
    forward = []
    for row_a in range(width_count):
        partial_sum = target[row_a]
        for prior in range(row_a):
            partial_sum = partial_sum - factor[row_a, prior] * forward[prior]
        forward.append(partial_sum / factor[row_a, row_a])
    backward = [None] * width_count
    for row_a in reversed(range(width_count)):
        partial_sum = forward[row_a]
        for later in range(row_a + 1, width_count):
            partial_sum = partial_sum - factor[later, row_a] * backward[later]
        backward[row_a] = partial_sum / factor[row_a, row_a]
    return backward


def body(
    forcing_right_side, earlier_warmth, matter_condition, compressed_slot_number, normal_draw_factor
):
    spreading_rate, volumetric_retention = medium_traits(earlier_warmth, matter_condition)
    padded_cond = padded_2(spreading_rate, (("gx", 0), ("gy", 1)), 1)
    links = [harmonic(spreading_rate, other) for other in beside_all(padded_cond, spreading_rate)]

    def operate(field):
        padded = padded_2(field, (("gx", 0), ("gy", 1)), 1)
        result = volumetric_retention * field
        for conductance, neighbour in zip(links, beside_all(padded, field)):
            result = result + conductance * (field - neighbour)
        return result

    def sketch_sum(field):
        return lax.psum(
            sketch_local(field, compressed_slot_number, normal_draw_factor), ("gx", "gy")
        )

    solution = jnp.zeros_like(forcing_right_side)
    residual = forcing_right_side
    sketched = sketch_sum(residual)
    scale_norm = jnp.sqrt(jnp.sum(sketched * sketched) + epsilon)
    basis_list = [residual / scale_norm]
    sketch_list = [sketched / scale_norm]
    image_list = []
    columns = []
    for column in range(BASIS):
        images = operate(basis_list[column])
        image_list.append(images)
        image_sketch = sketch_sum(images)
        stacked = jnp.stack(sketch_list, axis=1)
        coeffs = jnp.dot(stacked.T, image_sketch, precision=highest)
        reduced = images
        for prior in range(column + 1):
            reduced = reduced - coeffs[prior] * basis_list[prior]
        remainder = image_sketch - jnp.dot(stacked, coeffs, precision=highest)
        norm_next = jnp.sqrt(jnp.sum(remainder * remainder) + epsilon)
        columns.append(
            jnp.concatenate(
                [coeffs, norm_next[None], jnp.zeros((BASIS - column - 1,), jnp.float32)]
            )
        )
        if column + 1 < BASIS:
            basis_list.append(reduced / norm_next)
            sketch_list.append(remainder / norm_next)
    hess = jnp.stack(columns, axis=1)
    weights = solve_small(hess, scale_norm)
    for prior in range(BASIS):
        solution = solution + weights[prior] * basis_list[prior]
    residual = forcing_right_side - operate(solution)
    return (solution, residual)


def solution(mesh):
    return jax.shard_map(
        body,
        mesh=mesh,
        in_specs=(
            P(("parts", "gx"), "gy", None),
            P(("parts", "gx"), "gy", None),
            P(("parts", "gx"), "gy", None),
            P(("parts", "gx"), "gy", None),
            P(("parts", "gx"), "gy", None),
        ),
        out_specs=(P(("parts", "gx"), "gy", None), P(("parts", "gx"), "gy", None)),
        check_vma=False,
    )
```

profile of v0, /device:TPU:0, one launch (start us, length us, event | category | flops | bytes accessed | tf_op | source)
XLA Modules:
  0.0 187.6 jit_solution(5906491994559464097)
XLA Ops:
  1.8 7.4 %while.33 = (s32[]{:T(128)}, f32[128]{0:T(128)S(1)}, f32[4,8192]{1,0:T(4,128)S(1)}, s32[4,8192]{1,0:T(4,128)S(1)}, s32[]{:T(128)}, /*index=5*/s32[]{:T(128)}) while((s32[]{:T(128)}, f32[128]{0:T(128)S(1)}, f32[4,8192]{1,0:T(4,128)S(1)}, s32[4,8192]{1,0:T(4,128)S(1)}, s32[]{:T(128)}, /*index=5*/s32[]{:T(128)}) %tuple.88), condition=%wide.region_1.2_spmd.clone, body=%wide.region_0.1_spmd.clone.sunk | while | flops 13631747 | bytes 132183 | solution.py:71
  1.9 1.8 fusion.118
  3.8 1.8 fusion.118
  5.6 1.8 fusion.118
  7.5 1.8 fusion.118
  9.3 35.2 %psum.21 = f32[128]{0:T(128)S(1)} all-reduce(f32[128]{0:T(128)S(1)} %get-tuple-element.83), channel_id=1, replica_groups=mesh['parts'=2,'gx'=4,'gy'=4] {'gx','gy'}, use_global_device_ids=true, to_apply=%region_2.3 | all-reduce | flops 128 | bytes 1024 | tf_op jit(solution)/shard_map/psum | solution.py:110
  45.8 1.4 collective-permute-start.1
  47.3 3.0 %collective-permute-start.3 = (f32[1,8,1024]{2,1,0:T(8,128)S(1)}, f32[1,8,1024]{2,1,0:T(8,128)S(1)}, u32[]{:S(2)}, u32[]{:S(2)}) collective-permute-start(f32[1,8,1024]{2,1,0:T(8,128)S(1)} %get-tuple-element.182), channel_id=1, source_target_pairs={{0,4},{4,8},{8,12},{1,5},{5,9},{9,13},{2,6},{6,10},{10,14},{3,7},{... | collective-permute-start | bytes 98312 | tf_op jit(solution)/shard_map/ppermute | solution.py:21
  50.4 1.3 collective-permute-start
  51.7 3.0 %collective-permute-start.2 = (f32[1,8,1024]{2,1,0:T(8,128)S(1)}, f32[1,8,1024]{2,1,0:T(8,128)S(1)}, u32[]{:S(2)}, u32[]{:S(2)}) collective-permute-start(f32[1,8,1024]{2,1,0:T(8,128)S(1)} %get-tuple-element.180), channel_id=1, source_target_pairs={{0,4},{4,8},{8,12},{1,5},{5,9},{9,13},{2,6},{6,10},{10,14},{3,7},{... | collective-permute-start | bytes 98312 | tf_op jit(solution)/shard_map/ppermute | solution.py:21
  54.8 1.3 collective-permute-start.5
  56.1 4.5 %collective-permute-start.7 = (f32[6,1,1024]{2,1,0:T(1,128)S(1)}, f32[6,1,1024]{2,1,0:T(1,128)S(1)}, u32[]{:S(2)}, u32[]{:S(2)}) collective-permute-start(f32[6,1,1024]{2,1,0:T(1,128)S(1)} %get-tuple-element.175), channel_id=1, source_target_pairs={{0,1},{1,2},{2,3},{4,5},{5,6},{6,7},{8,9},{9,10},{10,11},{12,13},{... | collective-permute-start | bytes 73736 | tf_op jit(solution)/shard_map/ppermute | solution.py:21
  60.7 1.3 collective-permute-start.4
  62.0 4.5 %collective-permute-start.6 = (f32[6,1,1024]{2,1,0:T(1,128)S(1)}, f32[6,1,1024]{2,1,0:T(1,128)S(1)}, u32[]{:S(2)}, u32[]{:S(2)}) collective-permute-start(f32[6,1,1024]{2,1,0:T(1,128)S(1)} %get-tuple-element.173), channel_id=1, source_target_pairs={{0,1},{1,2},{2,3},{4,5},{5,6},{6,7},{8,9},{9,10},{10,11},{12,13},{... | collective-permute-start | bytes 73736 | tf_op jit(solution)/shard_map/ppermute | solution.py:21
  66.6 1.5 collective-permute-done.6
  68.5 7.4 %while.34 = (s32[]{:T(128)}, f32[128]{0:T(128)S(1)}, f32[4,8192]{1,0:T(4,128)S(1)}, s32[4,8192]{1,0:T(4,128)S(1)}, s32[]{:T(128)}, /*index=5*/s32[]{:T(128)}) while((s32[]{:T(128)}, f32[128]{0:T(128)S(1)}, f32[4,8192]{1,0:T(4,128)S(1)}, s32[4,8192]{1,0:T(4,128)S(1)}, s32[]{:T(128)}, /*index=5*/s32[]{:T(128)}) %tuple.89), condition=%wide.region_5.6_spmd.clone, body=%wide.region_4.5_spmd.clone.sunk | while | flops 13631747 | bytes 132183 | solution.py:71
  68.6 1.8 fusion.120
  70.5 1.8 fusion.120
  72.3 1.8 fusion.120
  74.2 1.8 fusion.120
  76.0 32.0 %psum.22 = f32[128]{0:T(128)S(1)} all-reduce(f32[128]{0:T(128)S(1)} %get-tuple-element.84), channel_id=1, replica_groups=mesh['parts'=2,'gx'=4,'gy'=4] {'gx','gy'}, use_global_device_ids=true, to_apply=%region_6.7 | all-reduce | flops 128 | bytes 1024 | tf_op jit(solution)/shard_map/psum | solution.py:110
  112.5 3.0 %collective-permute-start.9 = (f32[1,8,1024]{2,1,0:T(8,128)S(1)}, f32[1,8,1024]{2,1,0:T(8,128)S(1)}, u32[]{:S(2)}, u32[]{:S(2)}) collective-permute-start(f32[1,8,1024]{2,1,0:T(8,128)S(1)} %get-tuple-element.178), channel_id=1, source_target_pairs={{0,4},{4,8},{8,12},{1,5},{5,9},{9,13},{2,6},{6,10},{10,14},{3,7},{... | collective-permute-start | bytes 98312 | tf_op jit(solution)/shard_map/ppermute | solution.py:21
  117.7 4.5 %collective-permute-start.11 = (f32[6,1,1024]{2,1,0:T(1,128)S(1)}, f32[6,1,1024]{2,1,0:T(1,128)S(1)}, u32[]{:S(2)}, u32[]{:S(2)}) collective-permute-start(f32[6,1,1024]{2,1,0:T(1,128)S(1)} %get-tuple-element.171), channel_id=1, source_target_pairs={{0,1},{1,2},{2,3},{4,5},{5,6},{6,7},{8,9},{9,10},{10,11},{12,13},{... | collective-permute-start | bytes 73736 | tf_op jit(solution)/shard_map/ppermute | solution.py:21
  124.2 7.4 %while.35 = (s32[]{:T(128)}, f32[128]{0:T(128)S(1)}, f32[4,8192]{1,0:T(4,128)S(1)}, s32[4,8192]{1,0:T(4,128)S(1)}, s32[]{:T(128)}, /*index=5*/s32[]{:T(128)}) while((s32[]{:T(128)}, f32[128]{0:T(128)S(1)}, f32[4,8192]{1,0:T(4,128)S(1)}, s32[4,8192]{1,0:T(4,128)S(1)}, s32[]{:T(128)}, /*index=5*/s32[]{:T(128)}) %tuple.87), condition=%wide.region_9.10_spmd.clone, body=%wide.region_8.9_spmd.clone.sunk | while | flops 13631747 | bytes 132183 | solution.py:71
  124.3 1.8 fusion.122
  126.1 1.8 fusion.122
  128.0 1.8 fusion.122
  129.9 1.8 fusion.122
  131.7 32.0 %psum.23 = f32[128]{0:T(128)S(1)} all-reduce(f32[128]{0:T(128)S(1)} %get-tuple-element.85), channel_id=1, replica_groups=mesh['parts'=2,'gx'=4,'gy'=4] {'gx','gy'}, use_global_device_ids=true, to_apply=%region_10.11 | all-reduce | flops 128 | bytes 1024 | tf_op jit(solution)/shard_map/psum | solution.py:110
  175.3 3.0 %collective-permute-start.13 = (f32[1,8,1024]{2,1,0:T(8,128)S(1)}, f32[1,8,1024]{2,1,0:T(8,128)S(1)}, u32[]{:S(2)}, u32[]{:S(2)}) collective-permute-start(f32[1,8,1024]{2,1,0:T(8,128)S(1)} %get-tuple-element.176), channel_id=1, source_target_pairs={{0,4},{4,8},{8,12},{1,5},{5,9},{9,13},{2,6},{6,10},{10,14},{3,7},{... | collective-permute-start | bytes 98312 | tf_op jit(solution)/shard_map/ppermute | solution.py:21
  180.5 4.5 %collective-permute-start.15 = (f32[6,1,1024]{2,1,0:T(1,128)S(1)}, f32[6,1,1024]{2,1,0:T(1,128)S(1)}, u32[]{:S(2)}, u32[]{:S(2)}) collective-permute-start(f32[6,1,1024]{2,1,0:T(1,128)S(1)} %get-tuple-element.169), channel_id=1, source_target_pairs={{0,1},{1,2},{2,3},{4,5},{5,6},{6,7},{8,9},{9,10},{10,11},{12,13},{... | collective-permute-start | bytes 73736 | tf_op jit(solution)/shard_map/ppermute | solution.py:21
  185.1 1.5 collective-permute-done.15
  (82 shorter events, 19.7 us)
Async XLA Ops:
  0.6 1.1 copy-start
  0.7 1.1 copy-start.2
  45.8 4.5 %copy-start.4 = (s32[4,8,1024]{2,1,0:T(8,128)S(1)}, s32[4,8,1024]{2,1,0:T(8,128)}, u32[]{:S(2)}) copy-start(s32[4,8,1024]{2,1,0:T(8,128)} %param.13) | copy-start | bytes 393220
  45.8 4.5 %copy-start.3 = (f32[4,8,1024]{2,1,0:T(8,128)S(1)}, f32[4,8,1024]{2,1,0:T(8,128)}, u32[]{:S(2)}) copy-start(f32[4,8,1024]{2,1,0:T(8,128)} %param.12) | copy-start | bytes 393220
  45.8 8.9 %collective-permute-start.1 = (f32[1,8,1024]{2,1,0:T(8,128)S(1)}, f32[1,8,1024]{2,1,0:T(8,128)S(1)}, u32[]{:S(2)}, u32[]{:S(2)}) collective-permute-start(f32[1,8,1024]{2,1,0:T(8,128)S(1)} %get-tuple-element.183), channel_id=1, source_target_pairs={{4,0},{8,4},{12,8},{5,1},{9,5},{13,9},{6,2},{10,6},{14,10},{7,3},{... | collective-permute-start | bytes 98312 | tf_op jit(solution)/shard_map/ppermute | solution.py:24
  47.3 7.5 %collective-permute-start.3 = (f32[1,8,1024]{2,1,0:T(8,128)S(1)}, f32[1,8,1024]{2,1,0:T(8,128)S(1)}, u32[]{:S(2)}, u32[]{:S(2)}) collective-permute-start(f32[1,8,1024]{2,1,0:T(8,128)S(1)} %get-tuple-element.182), channel_id=1, source_target_pairs={{0,4},{4,8},{8,12},{1,5},{5,9},{9,13},{2,6},{6,10},{10,14},{3,7},{... | collective-permute-start | bytes 98312 | tf_op jit(solution)/shard_map/ppermute | solution.py:21
  50.4 10.3 %collective-permute-start = (f32[1,8,1024]{2,1,0:T(8,128)S(1)}, f32[1,8,1024]{2,1,0:T(8,128)S(1)}, u32[]{:S(2)}, u32[]{:S(2)}) collective-permute-start(f32[1,8,1024]{2,1,0:T(8,128)S(1)} %get-tuple-element.181), channel_id=1, source_target_pairs={{4,0},{8,4},{12,8},{5,1},{9,5},{13,9},{6,2},{10,6},{14,10},{7,3},{... | collective-permute-start | bytes 98312 | tf_op jit(solution)/shard_map/ppermute | solution.py:24
  51.7 9.0 %collective-permute-start.2 = (f32[1,8,1024]{2,1,0:T(8,128)S(1)}, f32[1,8,1024]{2,1,0:T(8,128)S(1)}, u32[]{:S(2)}, u32[]{:S(2)}) collective-permute-start(f32[1,8,1024]{2,1,0:T(8,128)S(1)} %get-tuple-element.180), channel_id=1, source_target_pairs={{0,4},{4,8},{8,12},{1,5},{5,9},{9,13},{2,6},{6,10},{10,14},{3,7},{... | collective-permute-start | bytes 98312 | tf_op jit(solution)/shard_map/ppermute | solution.py:21
  54.8 11.8 %collective-permute-start.5 = (f32[6,1,1024]{2,1,0:T(1,128)S(1)}, f32[6,1,1024]{2,1,0:T(1,128)S(1)}, u32[]{:S(2)}, u32[]{:S(2)}) collective-permute-start(f32[6,1,1024]{2,1,0:T(1,128)S(1)} %get-tuple-element.174), channel_id=1, source_target_pairs={{1,0},{2,1},{3,2},{5,4},{6,5},{7,6},{9,8},{10,9},{11,10},{13,12},{... | collective-permute-start | bytes 73736 | tf_op jit(solution)/shard_map/ppermute | solution.py:24
  56.1 10.5 %collective-permute-start.7 = (f32[6,1,1024]{2,1,0:T(1,128)S(1)}, f32[6,1,1024]{2,1,0:T(1,128)S(1)}, u32[]{:S(2)}, u32[]{:S(2)}) collective-permute-start(f32[6,1,1024]{2,1,0:T(1,128)S(1)} %get-tuple-element.175), channel_id=1, source_target_pairs={{0,1},{1,2},{2,3},{4,5},{5,6},{6,7},{8,9},{9,10},{10,11},{12,13},{... | collective-permute-start | bytes 73736 | tf_op jit(solution)/shard_map/ppermute | solution.py:21
  60.7 5.9 %collective-permute-start.4 = (f32[6,1,1024]{2,1,0:T(1,128)S(1)}, f32[6,1,1024]{2,1,0:T(1,128)S(1)}, u32[]{:S(2)}, u32[]{:S(2)}) collective-permute-start(f32[6,1,1024]{2,1,0:T(1,128)S(1)} %get-tuple-element.172), channel_id=1, source_target_pairs={{1,0},{2,1},{3,2},{5,4},{6,5},{7,6},{9,8},{10,9},{11,10},{13,12},{... | collective-permute-start | bytes 73736 | tf_op jit(solution)/shard_map/ppermute | solution.py:24
  62.0 6.1 %collective-permute-start.6 = (f32[6,1,1024]{2,1,0:T(1,128)S(1)}, f32[6,1,1024]{2,1,0:T(1,128)S(1)}, u32[]{:S(2)}, u32[]{:S(2)}) collective-permute-start(f32[6,1,1024]{2,1,0:T(1,128)S(1)} %get-tuple-element.173), channel_id=1, source_target_pairs={{0,1},{1,2},{2,3},{4,5},{5,6},{6,7},{8,9},{9,10},{10,11},{12,13},{... | collective-permute-start | bytes 73736 | tf_op jit(solution)/shard_map/ppermute | solution.py:21
  111.2 5.0 %collective-permute-start.8 = (f32[1,8,1024]{2,1,0:T(8,128)S(1)}, f32[1,8,1024]{2,1,0:T(8,128)S(1)}, u32[]{:S(2)}, u32[]{:S(2)}) collective-permute-start(f32[1,8,1024]{2,1,0:T(8,128)S(1)} %get-tuple-element.179), channel_id=1, source_target_pairs={{4,0},{8,4},{12,8},{5,1},{9,5},{13,9},{6,2},{10,6},{14,10},{7,3},{... | collective-permute-start | bytes 98312 | tf_op jit(solution)/shard_map/ppermute | solution.py:24
  112.5 3.9 %collective-permute-start.9 = (f32[1,8,1024]{2,1,0:T(8,128)S(1)}, f32[1,8,1024]{2,1,0:T(8,128)S(1)}, u32[]{:S(2)}, u32[]{:S(2)}) collective-permute-start(f32[1,8,1024]{2,1,0:T(8,128)S(1)} %get-tuple-element.178), channel_id=1, source_target_pairs={{0,4},{4,8},{8,12},{1,5},{5,9},{9,13},{2,6},{6,10},{10,14},{3,7},{... | collective-permute-start | bytes 98312 | tf_op jit(solution)/shard_map/ppermute | solution.py:21
  116.4 6.6 %collective-permute-start.10 = (f32[6,1,1024]{2,1,0:T(1,128)S(1)}, f32[6,1,1024]{2,1,0:T(1,128)S(1)}, u32[]{:S(2)}, u32[]{:S(2)}) collective-permute-start(f32[6,1,1024]{2,1,0:T(1,128)S(1)} %get-tuple-element.170), channel_id=1, source_target_pairs={{1,0},{2,1},{3,2},{5,4},{6,5},{7,6},{9,8},{10,9},{11,10},{13,12},{... | collective-permute-start | bytes 73736 | tf_op jit(solution)/shard_map/ppermute | solution.py:24
  117.7 6.1 %collective-permute-start.11 = (f32[6,1,1024]{2,1,0:T(1,128)S(1)}, f32[6,1,1024]{2,1,0:T(1,128)S(1)}, u32[]{:S(2)}, u32[]{:S(2)}) collective-permute-start(f32[6,1,1024]{2,1,0:T(1,128)S(1)} %get-tuple-element.171), channel_id=1, source_target_pairs={{0,1},{1,2},{2,3},{4,5},{5,6},{6,7},{8,9},{9,10},{10,11},{12,13},{... | collective-permute-start | bytes 73736 | tf_op jit(solution)/shard_map/ppermute | solution.py:21
  174.0 12.6 %copy-start.1 = (f32[4,8,1024]{2,1,0:T(8,128)}, f32[4,8,1024]{2,1,0:T(8,128)S(1)}, u32[]{:S(2)}) copy-start(f32[4,8,1024]{2,1,0:T(8,128)S(1)} %multiply_add_fusion) | copy-start | bytes 393220
  174.0 4.3 %collective-permute-start.12 = (f32[1,8,1024]{2,1,0:T(8,128)S(1)}, f32[1,8,1024]{2,1,0:T(8,128)S(1)}, u32[]{:S(2)}, u32[]{:S(2)}) collective-permute-start(f32[1,8,1024]{2,1,0:T(8,128)S(1)} %get-tuple-element.177), channel_id=1, source_target_pairs={{4,0},{8,4},{12,8},{5,1},{9,5},{13,9},{6,2},{10,6},{14,10},{7,3},{... | collective-permute-start | bytes 98312 | tf_op jit(solution)/shard_map/ppermute | solution.py:24
  175.3 3.9 %collective-permute-start.13 = (f32[1,8,1024]{2,1,0:T(8,128)S(1)}, f32[1,8,1024]{2,1,0:T(8,128)S(1)}, u32[]{:S(2)}, u32[]{:S(2)}) collective-permute-start(f32[1,8,1024]{2,1,0:T(8,128)S(1)} %get-tuple-element.176), channel_id=1, source_target_pairs={{0,4},{4,8},{8,12},{1,5},{5,9},{9,13},{2,6},{6,10},{10,14},{3,7},{... | collective-permute-start | bytes 98312 | tf_op jit(solution)/shard_map/ppermute | solution.py:21
  179.2 5.9 %collective-permute-start.14 = (f32[6,1,1024]{2,1,0:T(1,128)S(1)}, f32[6,1,1024]{2,1,0:T(1,128)S(1)}, u32[]{:S(2)}, u32[]{:S(2)}) collective-permute-start(f32[6,1,1024]{2,1,0:T(1,128)S(1)} %get-tuple-element.168), channel_id=1, source_target_pairs={{1,0},{2,1},{3,2},{5,4},{6,5},{7,6},{9,8},{10,9},{11,10},{13,12},{... | collective-permute-start | bytes 73736 | tf_op jit(solution)/shard_map/ppermute | solution.py:24
  180.5 6.1 %collective-permute-start.15 = (f32[6,1,1024]{2,1,0:T(1,128)S(1)}, f32[6,1,1024]{2,1,0:T(1,128)S(1)}, u32[]{:S(2)}, u32[]{:S(2)}) collective-permute-start(f32[6,1,1024]{2,1,0:T(1,128)S(1)} %get-tuple-element.169), channel_id=1, source_target_pairs={{0,1},{1,2},{2,3},{4,5},{5,6},{6,7},{8,9},{9,10},{10,11},{12,13},{... | collective-permute-start | bytes 73736 | tf_op jit(solution)/shard_map/ppermute | solution.py:21
where the time goes:
time: 191 us; the launch traced here: 188 us
  blocking collectives  99.2 us (52%)
  starting transfers between devices  40.8 us (21%)
  matrix products  22.6 us (12%)
  other arithmetic  8.73 us (5%)
  between operations  8.21 us (4%)
  waiting for transfers between devices  4.75 us (2%)
  local copies, waits for them, and re-layouts  2.96 us (2%)
    psum x3, blocking collectives, sketch_sum(): lax.psum(sketch_local(field, compressed_slot_number, normal_draw_factor),...  99.2 us
    ppermute x8, starting transfers between devices, padded_2(): lax.ppermute(lax.slice_in_dim(block, block.shape[dim] - width, None, axis...  30.3 us
    dot_general x12, matrix products, add_block(): return (totals + jnp.dot(block_vals, onehot, precision=highest), None)  21.6 us
    ppermute x8, starting transfers between devices, padded_2(): lax.ppermute(lax.slice_in_dim(block, 0, width, axis=dim), axis, backward)  10.5 us
    ppermute x8, waiting for transfers between devices, padded_2(): lax.ppermute(lax.slice_in_dim(block, block.shape[dim] - width, None, axis...  4.73 us
  transfers between devices with their start and end apart: 16, of which 5 were waited for; matrix products, arithmetic and copies ran while one was open for 1% of the time, Pallas kernels for 0%

commit v1 on v0

v1 whole, which is shorter than its diff:
```python
import functools

import jax
import jax.numpy as jnp
from jax import lax
from jax.experimental import pallas as pl
from jax.experimental.pallas import tpu as pltpu
from jax.sharding import PartitionSpec as P

SKETCH = 128
LOW = 16
HIGH = SKETCH // LOW
MESH = pl.DeviceIdType.MESH
epsilon = 1e-06
highest = lax.Precision.HIGHEST
f32 = jnp.float32
bf16 = jnp.bfloat16


def harmonic(first, second):
    return 2.0 * first * second / (first + second)


def total(field):
    return jnp.sum(jnp.sum(field, axis=1, keepdims=True), axis=0, keepdims=True)


def coefficients(s0, s1, s2):
    beta = jnp.sqrt(total(s0 * s0) + epsilon)
    inv_beta = 1.0 / beta
    q0 = s0 * inv_beta
    p0 = s1 * inv_beta
    h00 = total(q0 * p0)
    t0 = p0 - h00 * q0
    n0 = jnp.sqrt(total(t0 * t0) + epsilon)
    inv_n0 = 1.0 / n0
    q1 = t0 * inv_n0
    p1 = (s2 * inv_beta - h00 * p0) * inv_n0
    h01 = total(q0 * p1)
    h11 = total(q1 * p1)
    t1 = p1 - h01 * q0 - h11 * q1
    n1sq = total(t1 * t1) + epsilon
    m00 = h00 * h00 + n0 * n0
    m01 = h00 * h01 + n0 * h11
    m11 = h01 * h01 + h11 * h11 + n1sq
    b0 = beta * h00
    b1 = beta * h01
    l00 = jnp.sqrt(m00)
    l10 = m01 / l00
    l11 = jnp.sqrt(m11 - l10 * l10)
    f0 = b0 / l00
    f1 = (b1 - l10 * f0) / l11
    y1 = f1 / l11
    y0 = (f0 - l10 * y1) / l00
    c1 = y1 * inv_beta * inv_n0
    c0 = y0 * inv_beta - c1 * h00
    return c0, c1


def kernel(
    ngx, ngy, nx, ny, nz,
    f_hbm, w_hbm, m_hbm, s_hbm, d_hbm,
    z1, z2, c_out,
    r, w, m, slot, d, cond, cap, lx, ly, lylow, lz, onehot, wh, wl,
    hx_r, hx_c, hx_z, hy_rc, hy_z, py_rc, py_z,
    mine, gathered, load_sem, hs_sem, hr_sem, as_sem, ar_sem,
):
    gx = lax.axis_index("gx")
    gy = lax.axis_index("gy")
    count = ngx * ngy
    me = gx * ngy + gy

    loads = [
        pltpu.make_async_copy(src, dst, load_sem.at[i])
        for i, (src, dst) in enumerate(
            ((w_hbm, w), (m_hbm, m), (f_hbm, r), (s_hbm, slot), (d_hbm, d))
        )
    ]
    for load in loads:
        load.start()

    def peer(step):
        other = lax.rem(me + step, count)
        return {"gx": lax.div(other, ngy), "gy": lax.rem(other, ngy)}

    barrier = pltpu.get_barrier_semaphore()

    def greet(step, carry):
        pl.semaphore_signal(barrier, inc=1, device_id=peer(step), device_id_type=MESH)
        return carry

    lax.fori_loop(1, count, greet, 0)

    has_x = (gx > 0, gx < ngx - 1)
    has_y = (gy > 0, gy < ngy - 1)
    to_x = ({"gx": gx - 1, "gy": gy}, {"gx": gx + 1, "gy": gy})
    to_y = ({"gx": gx, "gy": gy - 1}, {"gx": gx, "gy": gy + 1})
    edge_x = (0, nx - 1)
    edge_y = (0, ny - 1)

    def remote(src, dst, index, side, target):
        return pltpu.make_async_remote_copy(
            src_ref=src,
            dst_ref=dst.at[1 - side],
            send_sem=hs_sem.at[index, side],
            recv_sem=hr_sem.at[index, 1 - side],
            device_id=target,
            device_id_type=MESH,
        )

    def x_copies(src, dst, index):
        return [(has_x[s], remote(src.at[edge_x[s]], dst, index, s, to_x[s])) for s in (0, 1)]

    def y_copies(src, dst, index):
        return [(has_y[s], remote(src.at[s], dst, index, s, to_y[s])) for s in (0, 1)]

    def begin(copies):
        for there, copy in copies:
            pl.when(there)(copy.start)

    def arrive(copies):
        for there, copy in copies:
            pl.when(there)(copy.wait_send)

    def recv_wait(dst, index, side, src, there, target):
        copy = pltpu.make_async_remote_copy(
            src_ref=src,
            dst_ref=dst.at[side],
            send_sem=hs_sem.at[index, side],
            recv_sem=hr_sem.at[index, side],
            device_id=target,
            device_id_type=MESH,
        )
        pl.when(there)(copy.wait_recv)

    loads[0].wait()
    loads[1].wait()
    for x in range(nx):
        phase = m[x]
        cond[x] = jnp.where(phase == 0, 0.2, jnp.where(phase == 1, 1.0, 0.6)).astype(f32) * (0.5 + w[x])
        cap[x] = jnp.where(phase == 0, 1.0, jnp.where(phase == 1, 2.0, 1.5)).astype(f32)
    loads[2].wait()
    for s in (0, 1):
        for x in range(nx):
            py_rc[s, pl.ds(x, 1), :] = r[x, pl.ds(edge_y[s], 1), :]
            py_rc[s, pl.ds(nx + x, 1), :] = cond[x, pl.ds(edge_y[s], 1), :]

        @pl.when(jnp.logical_not(has_x[s]))
        def _():
            hx_r[s] = jnp.zeros((ny, nz), f32)
            hx_c[s] = jnp.zeros((ny, nz), f32)
            hx_z[s] = jnp.zeros((ny, nz), f32)

        @pl.when(jnp.logical_not(has_y[s]))
        def _():
            hy_rc[s] = jnp.zeros((2 * nx, nz), f32)
            hy_z[s] = jnp.zeros((nx, nz), f32)

    pl.semaphore_wait(barrier, count - 1)
    first = x_copies(cond, hx_c, 0) + y_copies(py_rc, hy_rc, 1) + x_copies(r, hx_r, 2)
    begin(first)

    lane = lax.broadcasted_iota(jnp.int32, (ny, nz), 1)
    row = lax.broadcasted_iota(jnp.int32, (ny, nz), 0)
    row_high = lax.broadcasted_iota(jnp.int32, (HIGH, nz), 0)
    row_low = lax.broadcasted_iota(jnp.int32, (LOW, nz), 0)

    def spread(x_ref, x, y, rows):
        return jnp.broadcast_to(x_ref[x, pl.ds(y, 1), :], (rows, nz))

    for x in range(nx):
        here = cond[x]
        if x > 0:
            lx[x] = harmonic(cond[x - 1], here)
        lz[x] = jnp.where(lane == nz - 1, 0.0, harmonic(here, pltpu.roll(here, nz - 1, 1)))
    loads[3].wait()
    loads[4].wait()

    def build(x, carry):
        for y in range(ny):
            low = jnp.bitwise_and(spread(slot, x, y, LOW), LOW - 1)
            onehot[x, y] = jnp.where(low == row_low, 1.0, 0.0).astype(bf16)
        return carry

    lax.fori_loop(0, nx, build, 0)

    def sketch(field):
        for x in range(nx):
            weighted = d[x] * field[x]
            upper = weighted.astype(bf16).astype(f32)
            wh[x] = upper
            wl[x] = weighted - upper

        def add(x, sums):
            for y in range(ny):
                mask = lax.shift_right_logical(spread(slot, x, y, HIGH), 4) == row_high
                left = jnp.concatenate(
                    [
                        jnp.where(mask, spread(wh, x, y, HIGH), 0.0),
                        jnp.where(mask, spread(wl, x, y, HIGH), 0.0),
                    ],
                    axis=0,
                ).astype(bf16)
                sums = sums + lax.dot_general(
                    left, onehot[x, y], (((1,), (1,)), ((), ())), preferred_element_type=f32
                )
            return sums

        sums = lax.fori_loop(0, nx, add, jnp.zeros((2 * HIGH, LOW), f32))
        both = sums[:HIGH] + sums[HIGH:]
        lanes = lax.broadcasted_iota(jnp.int32, (LOW, SKETCH), 1)
        expand = jnp.where(
            jnp.bitwise_and(lanes, LOW - 1) == lax.broadcasted_iota(jnp.int32, (LOW, SKETCH), 0), 1.0, 0.0
        ).astype(f32)
        wide = jnp.dot(both, expand, precision=highest, preferred_element_type=f32)
        keep = lax.shift_right_logical(
            lax.broadcasted_iota(jnp.int32, (HIGH, SKETCH), 1), 4
        ) == lax.broadcasted_iota(jnp.int32, (HIGH, SKETCH), 0)
        return jnp.sum(jnp.where(keep, wide, 0.0), axis=0, keepdims=True)

    def apply(field, halo_x, halo_y, out):
        for x in range(nx):
            v = field[x]
            below = halo_x[0] if x == 0 else field[x - 1]
            above = halo_x[1] if x == nx - 1 else field[x + 1]
            acc = cap[x] * v + lx[x + 1] * (v - above) + lx[x] * (v - below)
            up = jnp.where(row == ny - 1, halo_y(1, x), pltpu.roll(v, ny - 1, 0))
            flux = ly[x] * (v - up)
            entering = lylow[pl.ds(x, 1), :] * (halo_y(0, x) - v[0:1, :])
            acc = acc + flux - jnp.where(row == 0, entering, pltpu.roll(flux, 1, 0))
            flux = lz[x] * (v - pltpu.roll(v, nz - 1, 1))
            out[x] = acc + flux - pltpu.roll(flux, 1, 1)

    mine[3:4, :] = jnp.zeros((1, SKETCH), f32)
    mine[0:1, :] = sketch(r)

    for s in (0, 1):
        recv_wait(hx_c, 0, s, cond.at[0], has_x[s], to_x[s])
        recv_wait(hy_rc, 1, s, py_rc.at[0], has_y[s], to_y[s])
        recv_wait(hx_r, 2, s, r.at[0], has_x[s], to_x[s])
    lx[0] = harmonic(hx_c[0], cond[0])
    lx[nx] = harmonic(cond[nx - 1], hx_c[1])
    for x in range(nx):
        here = cond[x]
        up = jnp.where(row == ny - 1, hy_rc[1, pl.ds(nx + x, 1), :], pltpu.roll(here, ny - 1, 0))
        ly[x] = harmonic(here, up)
        lylow[pl.ds(x, 1), :] = harmonic(hy_rc[0, pl.ds(nx + x, 1), :], here[0:1, :])
    apply(r, hx_r, lambda s, x: hy_rc[s, pl.ds(x, 1), :], z1)
    for s in (0, 1):
        for x in range(nx):
            py_z[s, pl.ds(x, 1), :] = z1[x, pl.ds(edge_y[s], 1), :]
    second = x_copies(z1, hx_z, 3) + y_copies(py_z, hy_z, 4)
    begin(second)
    mine[1:2, :] = sketch(z1)
    for s in (0, 1):
        recv_wait(hx_z, 3, s, z1.at[0], has_x[s], to_x[s])
        recv_wait(hy_z, 4, s, py_z.at[0], has_y[s], to_y[s])
    apply(z1, hx_z, lambda s, x: hy_z[s, pl.ds(x, 1), :], z2)
    mine[2:3, :] = sketch(z2)

    def share(step, carry):
        pltpu.make_async_remote_copy(
            src_ref=mine,
            dst_ref=gathered.at[me],
            send_sem=as_sem.at[step],
            recv_sem=ar_sem.at[me],
            device_id=peer(step),
            device_id_type=MESH,
        ).start()
        return carry

    lax.fori_loop(1, count, share, 0)
    gathered[me] = mine[...]
    arrive(first)
    arrive(second)

    def collect(step, carry):
        other = lax.rem(me + step, count)
        copy = pltpu.make_async_remote_copy(
            src_ref=mine,
            dst_ref=gathered.at[other],
            send_sem=as_sem.at[step],
            recv_sem=ar_sem.at[other],
            device_id=peer(step),
            device_id_type=MESH,
        )
        copy.wait_recv()
        copy.wait_send()
        return carry

    lax.fori_loop(1, count, collect, 0)
    summed = jnp.sum(gathered[...], axis=0)
    c0, c1 = coefficients(summed[0:1], summed[1:2], summed[2:3])
    c_out[0:1, :] = jnp.broadcast_to(c0, (1, SKETCH))
    c_out[1:2, :] = jnp.broadcast_to(c1, (1, SKETCH))


def body(ngx, ngy, f, w, m, s, d):
    nx, ny, nz = f.shape
    count = ngx * ngy
    vm = lambda shape, dtype=f32: pltpu.VMEM(shape, dtype)
    block = (nx, ny, nz)
    z1, z2, c = pl.pallas_call(
        functools.partial(kernel, ngx, ngy, nx, ny, nz),
        out_shape=(
            jax.ShapeDtypeStruct(block, f32),
            jax.ShapeDtypeStruct(block, f32),
            jax.ShapeDtypeStruct((2, SKETCH), f32),
        ),
        in_specs=[pl.BlockSpec(memory_space=pl.ANY)] * 5,
        out_specs=[pl.BlockSpec(memory_space=pltpu.VMEM)] * 3,
        scratch_shapes=[
            vm(block), vm(block), vm(block, jnp.int32), vm(block, jnp.int32), vm(block),
            vm(block), vm(block),
            vm((nx + 1, ny, nz)), vm(block), vm((nx, nz)), vm(block),
            vm((nx, ny, LOW, nz), bf16), vm(block), vm(block),
            vm((2, ny, nz)), vm((2, ny, nz)), vm((2, ny, nz)),
            vm((2, 2 * nx, nz)), vm((2, nx, nz)),
            vm((2, 2 * nx, nz)), vm((2, nx, nz)),
            vm((4, SKETCH)), vm((count, 4, SKETCH)),
            pltpu.SemaphoreType.DMA((5,)),
            pltpu.SemaphoreType.DMA((5, 2)),
            pltpu.SemaphoreType.DMA((5, 2)),
            pltpu.SemaphoreType.DMA((count,)),
            pltpu.SemaphoreType.DMA((count,)),
        ],
        compiler_params=pltpu.CompilerParams(collective_id=0, has_side_effects=True),
        name="sketched_gmres",
    )(f, w, m, s, d)
    c0 = c[0, 0]
    c1 = c[1, 0]
    return c0 * f + c1 * z1, f - c0 * z1 - c1 * z2


def solution(mesh):
    spec = P(("parts", "gx"), "gy", None)
    return jax.shard_map(
        functools.partial(body, mesh.shape["gx"], mesh.shape["gy"]),
        mesh=mesh,
        in_specs=(spec,) * 5,
        out_specs=(spec, spec),
        check_vma=False,
    )
```

time: 191 us -> 23.3 us (0.12); the launches traced: 188 us -> 23.1 us
  blocking collectives: 99.2 us -> 0 us
  starting transfers between devices: 40.8 us -> 0 us
  matrix products: 22.6 us -> 0 us
  Pallas kernels: 0 us -> 18.4 us
  between operations: 8.21 us -> 0.66 us
  other arithmetic: 8.73 us -> 2.88 us
  waiting for transfers between devices: 4.75 us -> 0 us
    psum x3 -> x0, blocking collectives: 99.2 us -> none  [sketch_sum(): lax.psum(sketch_local(field, compressed_slot_number, normal_draw_factor),...]
    ppermute x16 -> x0, starting transfers between devices: 40.8 us -> none  [the longest x8 30.3 us: padded_2(): lax.ppermute(lax.slice_in_dim(block, block.shape[dim] - width, None, axis...]
    dot_general x15 -> x0, matrix products: 22.6 us -> none  [the longest x12 21.6 us: add_block(): return (totals + jnp.dot(block_vals, onehot, precision=highest), None)]
    pallas_call x0 -> x1, Pallas kernels: none -> 18.4 us  [body(): pl.pallas_call(functools.partial(kernel, ngx, ngy, nx, ny, nz), out_shape...]
    ppermute x16 -> x0, waiting for transfers between devices: 4.75 us -> none  [the longest x8 4.73 us: padded_2(): lax.ppermute(lax.slice_in_dim(block, block.shape[dim] - width, None, axis...]
    another operation x7 -> x0, other arithmetic: 2.32 us -> none  [the longest x3 0.86 us: solve_small(): factor = jnp.linalg.cholesky(gram_matrix)]
  transfers between devices with their start and end apart: 16 -> 0, of which waited for: 5 -> 0; matrix products, arithmetic and copies ran while one was open for 1% -> 0% of each run, Pallas kernels for 0% -> 0%
where the time goes in v1:
time: 23.3 us; the launch traced here: 23.1 us
  Pallas kernels  18.4 us (79%)
  other arithmetic  2.88 us (12%)
  local copies, waits for them, and re-layouts  1.21 us (5%)
  between operations  0.66 us (3%)
    pallas_call x1, Pallas kernels, body(): pl.pallas_call(functools.partial(kernel, ngx, ngy, nx, ny, nz), out_shape...  18.4 us
    sub x1, other arithmetic, body(): return (c0 * f + c1 * z1, f - c0 * z1 - c1 * z2)  2.88 us
    unnamed x4, local copies, waits for them, and re-layouts  0.68 us
    slice x1, local copies, waits for them, and re-layouts, body(): c0 = c[0, 0]  0.53 us

profile of v1, /device:TPU:0, one launch (start us, length us, event | category | flops | bytes accessed | tf_op | source)
XLA Modules:
  0.0 23.1 jit_solution(10557229862876264278)
XLA Ops:
  0.6 0.0 copy-start
  0.6 18.4 %sketched_gmres.1 = (f32[4,8,1024]{2,1,0:T(8,128)}, f32[4,8,1024]{2,1,0:T(8,128)}, f32[2,128]{1,0:T(2,128)}) custom-call(f32[4,8,1024]{2,1,0:T(8,128)} %f_hbm.1, f32[4,8,1024]{2,1,0:T(8,128)} %w_hbm.1, s32[4,8,1024]{2,1,0:T(8,128)} %m_hbm.1, s32[4,8,1024]{2,1,0:T(8,128)} %s_hbm.1, f32[4,8,1024]{2,1,0:T(8,128)} %d_hbm.1), custom_call_target="tpu_custom_call" | custom-call | tf_op jit(solution)/shard_map/sketched_gmres/pallas_call | solution.py:303
  19.0 0.0 copy-start.1
  19.0 0.7 %copy-done.1 = f32[2,128]{1,0:T(2,128)S(1)} copy-done((f32[2,128]{1,0:T(2,128)S(1)}, f32[2,128]{1,0:T(2,128)}, u32[]{:S(2)}) %copy-start.1) | copy-done | bytes 1048
  19.7 0.5 %fusion = (f32[1,1]{1,0:T(1,128)}, f32[1,1]{1,0:T(1,128)}) fusion(f32[2,128]{1,0:T(2,128)S(1)} %copy-done.1), kind=kLoop, calls=%fused_computation.2 | loop fusion | bytes 16 | tf_op jit(solution)/shard_map/slice | solution.py:330
  20.2 0.0 copy-done
  20.2 2.9 %multiply_subtract_fusion = (f32[4,8,1024]{2,1,0:T(8,128)}, f32[4,8,1024]{2,1,0:T(8,128)}) fusion(f32[4,8,1024]{2,1,0:T(8,128)} %get-tuple-element.7, f32[4,8,1024]{2,1,0:T(8,128)S(1)} %copy-done, f32[4,8,1024]{2,1,0:T(8,128)} %get-tuple-element.6, f32[]{:T(128)} %bitcast.1, f32[]{:T(128)} %bitcast), kind=kLoop, calls=%fused_computation | loop fusion | flops 229376 | bytes 655368 | tf_op jit(solution)/shard_map/sub | solution.py:332
Async XLA Ops:
  0.6 19.6 %copy-start = (f32[4,8,1024]{2,1,0:T(8,128)S(1)}, f32[4,8,1024]{2,1,0:T(8,128)}, u32[]{:S(2)}) copy-start(f32[4,8,1024]{2,1,0:T(8,128)} %f_hbm.1) | copy-start | bytes 393220
  19.0 0.7 %copy-start.1 = (f32[2,128]{1,0:T(2,128)S(1)}, f32[2,128]{1,0:T(2,128)}, u32[]{:S(2)}) copy-start(f32[2,128]{1,0:T(2,128)} %get-tuple-element.5) | copy-start | bytes 3076

commit v2 on v1

--- a/solution.py
+++ b/solution.py
@@ -60,8 +60,8 @@
 def kernel(
     ngx, ngy, nx, ny, nz,
     f_hbm, w_hbm, m_hbm, s_hbm, d_hbm,
-    z1, z2, c_out,
-    r, w, m, slot, d, cond, cap, lx, ly, lylow, lz, onehot, wh, wl,
+    answer, rest,
+    z1, z2, r, w, m, slot, d, cond, cap, lx, ly, lylow, lz, onehot, wh, wl,
     hx_r, hx_c, hx_z, hy_rc, hy_z, py_rc, py_z,
     mine, gathered, load_sem, hs_sem, hr_sem, as_sem, ar_sem,
 ):
@@ -291,8 +291,9 @@
     lax.fori_loop(1, count, collect, 0)
     summed = jnp.sum(gathered[...], axis=0)
     c0, c1 = coefficients(summed[0:1], summed[1:2], summed[2:3])
-    c_out[0:1, :] = jnp.broadcast_to(c0, (1, SKETCH))
-    c_out[1:2, :] = jnp.broadcast_to(c1, (1, SKETCH))
+    for x in range(nx):
+        answer[x] = c0 * r[x] + c1 * z1[x]
+        rest[x] = r[x] - c0 * z1[x] - c1 * z2[x]
 
 
 def body(ngx, ngy, f, w, m, s, d):
@@ -300,16 +301,13 @@
     count = ngx * ngy
     vm = lambda shape, dtype=f32: pltpu.VMEM(shape, dtype)
     block = (nx, ny, nz)
-    z1, z2, c = pl.pallas_call(
+    return pl.pallas_call(
         functools.partial(kernel, ngx, ngy, nx, ny, nz),
-        out_shape=(
-            jax.ShapeDtypeStruct(block, f32),
-            jax.ShapeDtypeStruct(block, f32),
-            jax.ShapeDtypeStruct((2, SKETCH), f32),
-        ),
+        out_shape=(vm(block), vm(block)),
         in_specs=[pl.BlockSpec(memory_space=pl.ANY)] * 5,
-        out_specs=[pl.BlockSpec(memory_space=pltpu.VMEM)] * 3,
+        out_specs=[pl.BlockSpec(memory_space=pltpu.VMEM)] * 2,
         scratch_shapes=[
+            vm(block), vm(block),
             vm(block), vm(block), vm(block, jnp.int32), vm(block, jnp.int32), vm(block),
             vm(block), vm(block),
             vm((nx + 1, ny, nz)), vm(block), vm((nx, nz)), vm(block),
@@ -327,9 +325,6 @@
         compiler_params=pltpu.CompilerParams(collective_id=0, has_side_effects=True),
         name="sketched_gmres",
     )(f, w, m, s, d)
-    c0 = c[0, 0]
-    c1 = c[1, 0]
-    return c0 * f + c1 * z1, f - c0 * z1 - c1 * z2
 
 
 def solution(mesh):

time: 23.3 us -> 19.9 us (0.85)
  other arithmetic: 2.88 us -> 0 us
  Pallas kernels: 18.4 us -> 17.8 us
    sub x1 -> x0, other arithmetic: 2.88 us -> none  [body(): return (c0 * f + c1 * z1, f - c0 * z1 - c1 * z2)]
    unnamed x4 -> x2, local copies, waits for them, and re-layouts: 0.68 us -> 1.31 us
    pallas_call x1, Pallas kernels: 18.4 us -> 17.8 us  [body(): pl.pallas_call(functools.partial(kernel, ngx, ngy, nx, ny, nz), out_shape...]
    slice x1 -> x0, local copies, waits for them, and re-layouts: 0.53 us -> none  [body(): c0 = c[0, 0]]
where the time goes in v2:
time: 19.9 us; the launch traced here: 19.8 us
  Pallas kernels  17.8 us (89%)
  local copies, waits for them, and re-layouts  1.31 us (7%)
  between operations  0.64 us (3%)
    pallas_call x1, Pallas kernels, body(): pl.pallas_call(functools.partial(kernel, ngx, ngy, nx, ny, nz), out_shape...  17.8 us
    unnamed x2, local copies, waits for them, and re-layouts  1.31 us

profile of v2, /device:TPU:0, one launch (start us, length us, event | category | flops | bytes accessed | tf_op | source)
XLA Modules:
  0.0 19.8 jit_solution(13151594875052749421)
XLA Ops:
  0.6 17.8 %sketched_gmres.1 = (f32[4,8,1024]{2,1,0:T(8,128)S(1)}, f32[4,8,1024]{2,1,0:T(8,128)S(1)}) custom-call(f32[4,8,1024]{2,1,0:T(8,128)} %f_hbm.1, f32[4,8,1024]{2,1,0:T(8,128)} %w_hbm.1, s32[4,8,1024]{2,1,0:T(8,128)} %m_hbm.1, s32[4,8,1024]{2,1,0:T(8,128)} %s_hbm.1, f32[4,8,1024]{2,1,0:T(8,128)} %d_hbm.1), custom_call_target="tpu_custom_call" | custom-call | tf_op jit(solution)/shard_map/sketched_gmres/pallas_call | solution.py:304
  18.5 0.7 %copy.9 = f32[4,8,1024]{2,1,0:T(8,128)} copy(f32[4,8,1024]{2,1,0:T(8,128)S(1)} %get-tuple-element.2) | data formatting | bytes 262144
  19.1 0.7 %copy.10 = f32[4,8,1024]{2,1,0:T(8,128)} copy(f32[4,8,1024]{2,1,0:T(8,128)S(1)} %get-tuple-element.3) | data formatting | bytes 262144

commit v3 on v2

--- a/solution.py
+++ b/solution.py
@@ -61,8 +61,8 @@
     ngx, ngy, nx, ny, nz,
     f_hbm, w_hbm, m_hbm, s_hbm, d_hbm,
     answer, rest,
-    z1, z2, r, w, m, slot, d, cond, cap, lx, ly, lylow, lz, onehot, wh, wl,
-    hx_r, hx_c, hx_z, hy_rc, hy_z, py_rc, py_z,
+    z1, z2, r, w, m, slot, d, cond, cap, lx, ly, lylow, lz, onehot, wh, wl, rows,
+    hx_r, hx_c, hx_z, hx_s, hx_d, hy_rc, hy_z, hy_s, hy_d, py_rc, py_z, py_s, py_d,
     mine, gathered, load_sem, hs_sem, hr_sem, as_sem, ar_sem,
 ):
     gx = lax.axis_index("gx")
@@ -150,15 +150,29 @@
             hx_r[s] = jnp.zeros((ny, nz), f32)
             hx_c[s] = jnp.zeros((ny, nz), f32)
             hx_z[s] = jnp.zeros((ny, nz), f32)
+            hx_d[s] = jnp.zeros((ny, nz), f32)
+            hx_s[s] = jnp.zeros((ny, nz), jnp.int32)
 
         @pl.when(jnp.logical_not(has_y[s]))
         def _():
             hy_rc[s] = jnp.zeros((2 * nx, nz), f32)
             hy_z[s] = jnp.zeros((nx, nz), f32)
+            hy_d[s] = jnp.zeros((nx, nz), f32)
+            hy_s[s] = jnp.zeros((nx, nz), jnp.int32)
 
     pl.semaphore_wait(barrier, count - 1)
     first = x_copies(cond, hx_c, 0) + y_copies(py_rc, hy_rc, 1) + x_copies(r, hx_r, 2)
     begin(first)
+    loads[3].wait()
+    loads[4].wait()
+    for s in (0, 1):
+        for x in range(nx):
+            py_s[s, pl.ds(x, 1), :] = slot[x, pl.ds(edge_y[s], 1), :]
+            py_d[s, pl.ds(x, 1), :] = d[x, pl.ds(edge_y[s], 1), :]
+    for x in range(nx):
+        rows[x] = slot[x]
+    early = x_copies(slot, hx_s, 5) + y_copies(py_s, hy_s, 6) + x_copies(d, hx_d, 7) + y_copies(py_d, hy_d, 8)
+    begin(early)
 
     lane = lax.broadcasted_iota(jnp.int32, (ny, nz), 1)
     row = lax.broadcasted_iota(jnp.int32, (ny, nz), 0)
@@ -173,27 +187,28 @@
         if x > 0:
             lx[x] = harmonic(cond[x - 1], here)
         lz[x] = jnp.where(lane == nz - 1, 0.0, harmonic(here, pltpu.roll(here, nz - 1, 1)))
-    loads[3].wait()
-    loads[4].wait()
 
     def build(x, carry):
         for y in range(ny):
-            low = jnp.bitwise_and(spread(slot, x, y, LOW), LOW - 1)
+            slots = spread(rows, x, y, LOW)
+            low = jnp.bitwise_and(slots, LOW - 1)
             onehot[x, y] = jnp.where(low == row_low, 1.0, 0.0).astype(bf16)
         return carry
 
     lax.fori_loop(0, nx, build, 0)
 
-    def sketch(field):
-        for x in range(nx):
-            weighted = d[x] * field[x]
-            upper = weighted.astype(bf16).astype(f32)
-            wh[x] = upper
-            wl[x] = weighted - upper
+    def split(x, weighted):
+        upper = weighted.astype(bf16).astype(f32)
+        wh[x] = upper
+        wl[x] = weighted - upper
+
+    def sketch(planes, field):
+        for x in range(nx):
+            split(x, d[x] * field[x])
 
         def add(x, sums):
             for y in range(ny):
-                mask = lax.shift_right_logical(spread(slot, x, y, HIGH), 4) == row_high
+                mask = lax.shift_right_logical(spread(rows, x, y, HIGH), 4) == row_high
                 left = jnp.concatenate(
                     [
                         jnp.where(mask, spread(wh, x, y, HIGH), 0.0),
@@ -206,7 +221,7 @@
                 )
             return sums
 
-        sums = lax.fori_loop(0, nx, add, jnp.zeros((2 * HIGH, LOW), f32))
+        sums = lax.fori_loop(0, planes, add, jnp.zeros((2 * HIGH, LOW), f32))
         both = sums[:HIGH] + sums[HIGH:]
         lanes = lax.broadcasted_iota(jnp.int32, (LOW, SKETCH), 1)
         expand = jnp.where(
@@ -221,18 +236,25 @@
     def apply(field, halo_x, halo_y, out):
         for x in range(nx):
             v = field[x]
-            below = halo_x[0] if x == 0 else field[x - 1]
-            above = halo_x[1] if x == nx - 1 else field[x + 1]
-            acc = cap[x] * v + lx[x + 1] * (v - above) + lx[x] * (v - below)
-            up = jnp.where(row == ny - 1, halo_y(1, x), pltpu.roll(v, ny - 1, 0))
+            if x == 0:
+                low = v if halo_x is None else v - halo_x[0]
+            else:
+                low = v - field[x - 1]
+            if x == nx - 1:
+                top = v if halo_x is None else v - halo_x[1]
+            else:
+                top = v - field[x + 1]
+            acc = cap[x] * v + lx[x + 1] * top + lx[x] * low
+            first_row, last_row = (0.0, 0.0) if halo_y is None else (halo_y(0, x), halo_y(1, x))
+            up = jnp.where(row == ny - 1, last_row, pltpu.roll(v, ny - 1, 0))
             flux = ly[x] * (v - up)
-            entering = lylow[pl.ds(x, 1), :] * (halo_y(0, x) - v[0:1, :])
+            entering = lylow[pl.ds(x, 1), :] * (first_row - v[0:1, :])
             acc = acc + flux - jnp.where(row == 0, entering, pltpu.roll(flux, 1, 0))
             flux = lz[x] * (v - pltpu.roll(v, nz - 1, 1))
             out[x] = acc + flux - pltpu.roll(flux, 1, 1)
 
     mine[3:4, :] = jnp.zeros((1, SKETCH), f32)
-    mine[0:1, :] = sketch(r)
+    mine[0:1, :] = sketch(nx, r)
 
     for s in (0, 1):
         recv_wait(hx_c, 0, s, cond.at[0], has_x[s], to_x[s])
@@ -251,12 +273,30 @@
             py_z[s, pl.ds(x, 1), :] = z1[x, pl.ds(edge_y[s], 1), :]
     second = x_copies(z1, hx_z, 3) + y_copies(py_z, hy_z, 4)
     begin(second)
-    mine[1:2, :] = sketch(z1)
-    for s in (0, 1):
-        recv_wait(hx_z, 3, s, z1.at[0], has_x[s], to_x[s])
-        recv_wait(hy_z, 4, s, py_z.at[0], has_y[s], to_y[s])
-    apply(z1, hx_z, lambda s, x: hy_z[s, pl.ds(x, 1), :], z2)
-    mine[2:3, :] = sketch(z2)
+    mine[1:2, :] = sketch(nx, z1)
+    for s in (0, 1):
+        recv_wait(hx_s, 5, s, slot.at[0], has_x[s], to_x[s])
+        recv_wait(hy_s, 6, s, py_s.at[0], has_y[s], to_y[s])
+        recv_wait(hx_d, 7, s, d.at[0], has_x[s], to_x[s])
+        recv_wait(hy_d, 8, s, py_d.at[0], has_y[s], to_y[s])
+        rows[nx + s] = hx_s[s]
+        split(nx + s, -lx[nx * s] * z1[edge_x[s]] * hx_d[s])
+        edge = []
+        for x in range(nx):
+            link = lylow[pl.ds(x, 1), :] if s == 0 else ly[x, pl.ds(ny - 1, 1), :]
+            edge.append(-link * z1[x, pl.ds(edge_y[s], 1), :] * hy_d[s, pl.ds(x, 1), :])
+            rows[nx + 2, pl.ds(s * nx + x, 1), :] = hy_s[s, pl.ds(x, 1), :]
+        edge = jnp.concatenate(edge, axis=0)
+        upper = edge.astype(bf16).astype(f32)
+        wh[nx + 2, pl.ds(s * nx, nx), :] = upper
+        wl[nx + 2, pl.ds(s * nx, nx), :] = edge - upper
+    for y in range(2 * nx, ny):
+        rows[nx + 2, pl.ds(y, 1), :] = jnp.zeros((1, nz), jnp.int32)
+        wh[nx + 2, pl.ds(y, 1), :] = jnp.zeros((1, nz), f32)
+        wl[nx + 2, pl.ds(y, 1), :] = jnp.zeros((1, nz), f32)
+    lax.fori_loop(nx, nx + 3, build, 0)
+    apply(z1, None, None, z2)
+    mine[2:3, :] = sketch(nx + 3, z2)
 
     def share(step, carry):
         pltpu.make_async_remote_copy(
@@ -272,7 +312,16 @@
     lax.fori_loop(1, count, share, 0)
     gathered[me] = mine[...]
     arrive(first)
+    arrive(early)
     arrive(second)
+    for s in (0, 1):
+        recv_wait(hx_z, 3, s, z1.at[0], has_x[s], to_x[s])
+        recv_wait(hy_z, 4, s, py_z.at[0], has_y[s], to_y[s])
+        z2[edge_x[s]] = z2[edge_x[s]] - lx[nx * s] * hx_z[s]
+        for x in range(nx):
+            link = lylow[pl.ds(x, 1), :] if s == 0 else ly[x, pl.ds(ny - 1, 1), :]
+            at = (x, pl.ds(edge_y[s], 1), slice(None))
+            z2[at] = z2[at] - link * hy_z[s, pl.ds(x, 1), :]
 
     def collect(step, carry):
         other = lax.rem(me + step, count)
@@ -301,6 +350,8 @@
     count = ngx * ngy
     vm = lambda shape, dtype=f32: pltpu.VMEM(shape, dtype)
     block = (nx, ny, nz)
+    wide = (nx + 3, ny, nz)
+    assert 2 * nx <= ny
     return pl.pallas_call(
         functools.partial(kernel, ngx, ngy, nx, ny, nz),
         out_shape=(vm(block), vm(block)),
@@ -311,14 +362,14 @@
             vm(block), vm(block), vm(block, jnp.int32), vm(block, jnp.int32), vm(block),
             vm(block), vm(block),
             vm((nx + 1, ny, nz)), vm(block), vm((nx, nz)), vm(block),
-            vm((nx, ny, LOW, nz), bf16), vm(block), vm(block),
-            vm((2, ny, nz)), vm((2, ny, nz)), vm((2, ny, nz)),
-            vm((2, 2 * nx, nz)), vm((2, nx, nz)),
-            vm((2, 2 * nx, nz)), vm((2, nx, nz)),
+            vm((nx + 3, ny, LOW, nz), bf16), vm(wide), vm(wide), vm(wide, jnp.int32),
+            vm((2, ny, nz)), vm((2, ny, nz)), vm((2, ny, nz)), vm((2, ny, nz), jnp.int32), vm((2, ny, nz)),
+            vm((2, 2 * nx, nz)), vm((2, nx, nz)), vm((2, nx, nz), jnp.int32), vm((2, nx, nz)),
+            vm((2, 2 * nx, nz)), vm((2, nx, nz)), vm((2, nx, nz), jnp.int32), vm((2, nx, nz)),
             vm((4, SKETCH)), vm((count, 4, SKETCH)),
             pltpu.SemaphoreType.DMA((5,)),
-            pltpu.SemaphoreType.DMA((5, 2)),
-            pltpu.SemaphoreType.DMA((5, 2)),
+            pltpu.SemaphoreType.DMA((9, 2)),
+            pltpu.SemaphoreType.DMA((9, 2)),
             pltpu.SemaphoreType.DMA((count,)),
             pltpu.SemaphoreType.DMA((count,)),
         ],

time: 19.9 us -> 19.2 us (0.965)
  Pallas kernels: 17.8 us -> 17.1 us
    pallas_call x1, Pallas kernels: 17.8 us -> 17.1 us  [body(): pl.pallas_call(functools.partial(kernel, ngx, ngy, nx, ny, nz), out_shape...]
where the time goes in v3:
time: 19.2 us; the launch traced here: 19.1 us
  Pallas kernels  17.1 us (89%)
  local copies, waits for them, and re-layouts  1.31 us (7%)
  between operations  0.64 us (3%)
    pallas_call x1, Pallas kernels, body(): pl.pallas_call(functools.partial(kernel, ngx, ngy, nx, ny, nz), out_shape...  17.1 us
    unnamed x2, local copies, waits for them, and re-layouts  1.31 us

profile of v3, /device:TPU:0, one launch (start us, length us, event | category | flops | bytes accessed | tf_op | source)
XLA Modules:
  0.0 19.1 jit_solution(9445247291869867620)
XLA Ops:
  0.6 17.1 %sketched_gmres.1 = (f32[4,8,1024]{2,1,0:T(8,128)S(1)}, f32[4,8,1024]{2,1,0:T(8,128)S(1)}) custom-call(f32[4,8,1024]{2,1,0:T(8,128)} %f_hbm.1, f32[4,8,1024]{2,1,0:T(8,128)} %w_hbm.1, s32[4,8,1024]{2,1,0:T(8,128)} %m_hbm.1, s32[4,8,1024]{2,1,0:T(8,128)} %s_hbm.1, f32[4,8,1024]{2,1,0:T(8,128)} %d_hbm.1), custom_call_target="tpu_custom_call" | custom-call | tf_op jit(solution)/shard_map/sketched_gmres/pallas_call | solution.py:355
  17.8 0.7 %copy.9 = f32[4,8,1024]{2,1,0:T(8,128)} copy(f32[4,8,1024]{2,1,0:T(8,128)S(1)} %get-tuple-element.2) | data formatting | bytes 262144
  18.4 0.7 %copy.10 = f32[4,8,1024]{2,1,0:T(8,128)} copy(f32[4,8,1024]{2,1,0:T(8,128)S(1)} %get-tuple-element.3) | data formatting | bytes 262144

commit v4 on v3

--- a/solution.py
+++ b/solution.py
@@ -63,7 +63,7 @@
     answer, rest,
     z1, z2, r, w, m, slot, d, cond, cap, lx, ly, lylow, lz, onehot, wh, wl, rows,
     hx_r, hx_c, hx_z, hx_s, hx_d, hy_rc, hy_z, hy_s, hy_d, py_rc, py_z, py_s, py_d,
-    mine, gathered, load_sem, hs_sem, hr_sem, as_sem, ar_sem,
+    mine, gathered, load_sem, hs_sem, hr_sem, as_sem, ar_sem, known,
 ):
     gx = lax.axis_index("gx")
     gy = lax.axis_index("gy")
@@ -85,16 +85,34 @@
 
     barrier = pltpu.get_barrier_semaphore()
 
-    def greet(step, carry):
-        pl.semaphore_signal(barrier, inc=1, device_id=peer(step), device_id_type=MESH)
-        return carry
-
-    lax.fori_loop(1, count, greet, 0)
+    for step in range(1, ngx):
+        other = {"gx": lax.rem(gx + step, ngx), "gy": gy}
+        pl.semaphore_signal(barrier, inc=1, device_id=other, device_id_type=MESH)
 
     has_x = (gx > 0, gx < ngx - 1)
     has_y = (gy > 0, gy < ngy - 1)
     to_x = ({"gx": gx - 1, "gy": gy}, {"gx": gx + 1, "gy": gy})
     to_y = ({"gx": gx, "gy": gy - 1}, {"gx": gx, "gy": gy + 1})
+    for s in (0, 1):
+
+        @pl.when(has_y[s])
+        def _():
+            pl.semaphore_signal(barrier, inc=1, device_id=to_y[s], device_id_type=MESH)
+
+    def tell(turn):
+        for s in (0, 1):
+
+            @pl.when(has_y[s])
+            def _():
+                pl.semaphore_signal(known.at[turn, 1 - s], inc=1, device_id=to_y[s], device_id_type=MESH)
+
+    def hear(turn):
+        for s in (0, 1):
+
+            @pl.when(has_y[s])
+            def _():
+                pl.semaphore_wait(known.at[turn, s], 1)
+
     edge_x = (0, nx - 1)
     edge_y = (0, ny - 1)
 
@@ -160,7 +178,7 @@
             hy_d[s] = jnp.zeros((nx, nz), f32)
             hy_s[s] = jnp.zeros((nx, nz), jnp.int32)
 
-    pl.semaphore_wait(barrier, count - 1)
+    pl.semaphore_wait(barrier, ngx - 1 + has_y[0].astype(jnp.int32) + has_y[1].astype(jnp.int32))
     first = x_copies(cond, hx_c, 0) + y_copies(py_rc, hy_rc, 1) + x_copies(r, hx_r, 2)
     begin(first)
     loads[3].wait()
@@ -173,6 +191,8 @@
         rows[x] = slot[x]
     early = x_copies(slot, hx_s, 5) + y_copies(py_s, hy_s, 6) + x_copies(d, hx_d, 7) + y_copies(py_d, hy_d, 8)
     begin(early)
+    if ngy > 1:
+        tell(1)
 
     lane = lax.broadcasted_iota(jnp.int32, (ny, nz), 1)
     row = lax.broadcasted_iota(jnp.int32, (ny, nz), 0)
@@ -255,6 +275,9 @@
 
     mine[3:4, :] = jnp.zeros((1, SKETCH), f32)
     mine[0:1, :] = sketch(nx, r)
+    if ngy > 2:
+        hear(1)
+        tell(2)
 
     for s in (0, 1):
         recv_wait(hx_c, 0, s, cond.at[0], has_x[s], to_x[s])
@@ -273,6 +296,9 @@
             py_z[s, pl.ds(x, 1), :] = z1[x, pl.ds(edge_y[s], 1), :]
     second = x_copies(z1, hx_z, 3) + y_copies(py_z, hy_z, 4)
     begin(second)
+    for turn in range(3, ngy):
+        hear(turn - 1)
+        tell(turn)
     mine[1:2, :] = sketch(nx, z1)
     for s in (0, 1):
         recv_wait(hx_s, 5, s, slot.at[0], has_x[s], to_x[s])
@@ -309,6 +335,8 @@
         ).start()
         return carry
 
+    if ngy > 1:
+        hear(ngy - 1)
     lax.fori_loop(1, count, share, 0)
     gathered[me] = mine[...]
     arrive(first)
@@ -345,6 +373,15 @@
         rest[x] = r[x] - c0 * z1[x] - c1 * z2[x]
 
 
+def put_out(answer, rest, answer_out, rest_out, sem):
+    one = pltpu.make_async_copy(answer, answer_out, sem.at[0])
+    two = pltpu.make_async_copy(rest, rest_out, sem.at[1])
+    one.start()
+    two.start()
+    one.wait()
+    two.wait()
+
+
 def body(ngx, ngy, f, w, m, s, d):
     nx, ny, nz = f.shape
     count = ngx * ngy
@@ -352,7 +389,7 @@
     block = (nx, ny, nz)
     wide = (nx + 3, ny, nz)
     assert 2 * nx <= ny
-    return pl.pallas_call(
+    answer, rest = pl.pallas_call(
         functools.partial(kernel, ngx, ngy, nx, ny, nz),
         out_shape=(vm(block), vm(block)),
         in_specs=[pl.BlockSpec(memory_space=pl.ANY)] * 5,
@@ -372,10 +409,19 @@
             pltpu.SemaphoreType.DMA((9, 2)),
             pltpu.SemaphoreType.DMA((count,)),
             pltpu.SemaphoreType.DMA((count,)),
+            pltpu.SemaphoreType.REGULAR((ngy, 2)),
         ],
         compiler_params=pltpu.CompilerParams(collective_id=0, has_side_effects=True),
         name="sketched_gmres",
     )(f, w, m, s, d)
+    return pl.pallas_call(
+        put_out,
+        out_shape=(jax.ShapeDtypeStruct(block, f32), jax.ShapeDtypeStruct(block, f32)),
+        in_specs=[pl.BlockSpec(memory_space=pltpu.VMEM)] * 2,
+        out_specs=[pl.BlockSpec(memory_space=pl.ANY)] * 2,
+        scratch_shapes=[pltpu.SemaphoreType.DMA((2,))],
+        name="put_out",
+    )(pltpu.with_memory_space_constraint(answer, pltpu.VMEM), pltpu.with_memory_space_constraint(rest, pltpu.VMEM))
 
 
 def solution(mesh):

time: 19.2 us -> 18.1 us (0.943)
  local copies, waits for them, and re-layouts: 1.31 us -> 0 us
  Pallas kernels: 17.1 us -> 17.3 us
    unnamed x2 -> x0, local copies, waits for them, and re-layouts: 1.31 us -> none
    pallas_call x0 -> x1, Pallas kernels: none -> 0.72 us  [body(): pl.pallas_call(put_out, out_shape=(jax.ShapeDtypeStruct(block, f32), jax....]
    pallas_call x1, Pallas kernels: 17.1 us -> 16.6 us  [body(): pl.pallas_call(functools.partial(kernel, ngx, ngy, nx, ny, nz), out_shape...]
where the time goes in v4:
time: 18.1 us; the launch traced here: 18 us
  Pallas kernels  17.3 us (96%)
  between operations  0.64 us (4%)
    pallas_call x1, Pallas kernels, body(): pl.pallas_call(functools.partial(kernel, ngx, ngy, nx, ny, nz), out_shape...  16.6 us
    pallas_call x1, Pallas kernels, body(): pl.pallas_call(put_out, out_shape=(jax.ShapeDtypeStruct(block, f32), jax....  0.72 us

profile of v4, /device:TPU:0, one launch (start us, length us, event | category | flops | bytes accessed | tf_op | source)
XLA Modules:
  0.0 18.0 jit_solution(15609499595431357398)
XLA Ops:
  0.6 16.6 %sketched_gmres.1 = (f32[4,8,1024]{2,1,0:T(8,128)S(1)}, f32[4,8,1024]{2,1,0:T(8,128)S(1)}) custom-call(f32[4,8,1024]{2,1,0:T(8,128)} %f_hbm.1, f32[4,8,1024]{2,1,0:T(8,128)} %w_hbm.1, s32[4,8,1024]{2,1,0:T(8,128)} %m_hbm.1, s32[4,8,1024]{2,1,0:T(8,128)} %s_hbm.1, f32[4,8,1024]{2,1,0:T(8,128)} %d_hbm.1), custom_call_target="tpu_custom_call" | custom-call | tf_op jit(solution)/shard_map/sketched_gmres/pallas_call | solution.py:392
  17.3 0.7 %put_out.1 = (f32[4,8,1024]{2,1,0:T(8,128)}, f32[4,8,1024]{2,1,0:T(8,128)}) custom-call(f32[4,8,1024]{2,1,0:T(8,128)S(1)} %get-tuple-element.4.answer, f32[4,8,1024]{2,1,0:T(8,128)S(1)} %get-tuple-element.5.rest), custom_call_target="tpu_custom_call" | custom-call | tf_op jit(solution)/shard_map/put_out/pallas_call | solution.py:417

commit v5 on v4

--- a/solution.py
+++ b/solution.py
@@ -61,7 +61,7 @@
     ngx, ngy, nx, ny, nz,
     f_hbm, w_hbm, m_hbm, s_hbm, d_hbm,
     answer, rest,
-    z1, z2, r, w, m, slot, d, cond, cap, lx, ly, lylow, lz, onehot, wh, wl, rows,
+    z1, z2, r, w, m, slot, d, cond, cap, lx, ly, lylow, lz, onehot, wh, wl, wh1, wl1, rows,
     hx_r, hx_c, hx_z, hx_s, hx_d, hy_rc, hy_z, hy_s, hy_d, py_rc, py_z, py_s, py_d,
     mine, gathered, load_sem, hs_sem, hr_sem, as_sem, ar_sem, known,
 ):
@@ -222,26 +222,21 @@
         wh[x] = upper
         wl[x] = weighted - upper
 
-    def sketch(planes, field):
-        for x in range(nx):
-            split(x, d[x] * field[x])
-
+    def adder(parts):
         def add(x, sums):
             for y in range(ny):
                 mask = lax.shift_right_logical(spread(rows, x, y, HIGH), 4) == row_high
                 left = jnp.concatenate(
-                    [
-                        jnp.where(mask, spread(wh, x, y, HIGH), 0.0),
-                        jnp.where(mask, spread(wl, x, y, HIGH), 0.0),
-                    ],
-                    axis=0,
+                    [jnp.where(mask, spread(part, x, y, HIGH), 0.0) for part in parts], axis=0
                 ).astype(bf16)
                 sums = sums + lax.dot_general(
                     left, onehot[x, y], (((1,), (1,)), ((), ())), preferred_element_type=f32
                 )
             return sums
 
-        sums = lax.fori_loop(0, planes, add, jnp.zeros((2 * HIGH, LOW), f32))
+        return add
+
+    def finish(sums):
         both = sums[:HIGH] + sums[HIGH:]
         lanes = lax.broadcasted_iota(jnp.int32, (LOW, SKETCH), 1)
         expand = jnp.where(
@@ -274,7 +269,9 @@
             out[x] = acc + flux - pltpu.roll(flux, 1, 1)
 
     mine[3:4, :] = jnp.zeros((1, SKETCH), f32)
-    mine[0:1, :] = sketch(nx, r)
+    for x in range(nx):
+        split(x, d[x] * r[x])
+    mine[0:1, :] = finish(lax.fori_loop(0, nx, adder((wh, wl)), jnp.zeros((2 * HIGH, LOW), f32)))
     if ngy > 2:
         hear(1)
         tell(2)
@@ -299,7 +296,14 @@
     for turn in range(3, ngy):
         hear(turn - 1)
         tell(turn)
-    mine[1:2, :] = sketch(nx, z1)
+    apply(z1, None, None, z2)
+    for x in range(nx):
+        weighted = d[x] * z1[x]
+        upper = weighted.astype(bf16).astype(f32)
+        wh1[x] = upper
+        wl1[x] = weighted - upper
+        split(x, d[x] * z2[x])
+    sums = lax.fori_loop(0, nx, adder((wh1, wl1, wh, wl)), jnp.zeros((4 * HIGH, LOW), f32))
     for s in (0, 1):
         recv_wait(hx_s, 5, s, slot.at[0], has_x[s], to_x[s])
         recv_wait(hy_s, 6, s, py_s.at[0], has_y[s], to_y[s])
@@ -321,8 +325,9 @@
         wh[nx + 2, pl.ds(y, 1), :] = jnp.zeros((1, nz), f32)
         wl[nx + 2, pl.ds(y, 1), :] = jnp.zeros((1, nz), f32)
     lax.fori_loop(nx, nx + 3, build, 0)
-    apply(z1, None, None, z2)
-    mine[2:3, :] = sketch(nx + 3, z2)
+    halo_sums = lax.fori_loop(nx, nx + 3, adder((wh, wl)), jnp.zeros((2 * HIGH, LOW), f32))
+    mine[1:2, :] = finish(sums[: 2 * HIGH])
+    mine[2:3, :] = finish(sums[2 * HIGH :] + halo_sums)
 
     def share(step, carry):
         pltpu.make_async_remote_copy(
@@ -399,7 +404,7 @@
             vm(block), vm(block), vm(block, jnp.int32), vm(block, jnp.int32), vm(block),
             vm(block), vm(block),
             vm((nx + 1, ny, nz)), vm(block), vm((nx, nz)), vm(block),
-            vm((nx + 3, ny, LOW, nz), bf16), vm(wide), vm(wide), vm(wide, jnp.int32),
+            vm((nx + 3, ny, LOW, nz), bf16), vm(wide), vm(wide), vm(block), vm(block), vm(wide, jnp.int32),
             vm((2, ny, nz)), vm((2, ny, nz)), vm((2, ny, nz)), vm((2, ny, nz), jnp.int32), vm((2, ny, nz)),
             vm((2, 2 * nx, nz)), vm((2, nx, nz)), vm((2, nx, nz), jnp.int32), vm((2, nx, nz)),
             vm((2, 2 * nx, nz)), vm((2, nx, nz)), vm((2, nx, nz), jnp.int32), vm((2, nx, nz)),

time: 18.1 us -> 17.2 us (0.950)
  Pallas kernels: 17.3 us -> 16.4 us
    pallas_call x1, Pallas kernels: 16.6 us -> 15.7 us  [body(): pl.pallas_call(functools.partial(kernel, ngx, ngy, nx, ny, nz), out_shape...]
where the time goes in v5:
time: 17.2 us; the launch traced here: 17.1 us
  Pallas kernels  16.4 us (95%)
  between operations  0.64 us (4%)
    pallas_call x1, Pallas kernels, body(): pl.pallas_call(functools.partial(kernel, ngx, ngy, nx, ny, nz), out_shape...  15.7 us
    pallas_call x1, Pallas kernels, body(): pl.pallas_call(put_out, out_shape=(jax.ShapeDtypeStruct(block, f32), jax....  0.72 us

profile of v5, /device:TPU:0, one launch (start us, length us, event | category | flops | bytes accessed | tf_op | source)
XLA Modules:
  0.0 17.1 jit_solution(8216243121625963552)
XLA Ops:
  0.6 15.7 %sketched_gmres.1 = (f32[4,8,1024]{2,1,0:T(8,128)S(1)}, f32[4,8,1024]{2,1,0:T(8,128)S(1)}) custom-call(f32[4,8,1024]{2,1,0:T(8,128)} %f_hbm.1, f32[4,8,1024]{2,1,0:T(8,128)} %w_hbm.1, s32[4,8,1024]{2,1,0:T(8,128)} %m_hbm.1, s32[4,8,1024]{2,1,0:T(8,128)} %s_hbm.1, f32[4,8,1024]{2,1,0:T(8,128)} %d_hbm.1), custom_call_target="tpu_custom_call" | custom-call | tf_op jit(solution)/shard_map/sketched_gmres/pallas_call | solution.py:397
  16.3 0.7 %put_out.1 = (f32[4,8,1024]{2,1,0:T(8,128)}, f32[4,8,1024]{2,1,0:T(8,128)}) custom-call(f32[4,8,1024]{2,1,0:T(8,128)S(1)} %get-tuple-element.4.answer, f32[4,8,1024]{2,1,0:T(8,128)S(1)} %get-tuple-element.5.rest), custom_call_target="tpu_custom_call" | custom-call | tf_op jit(solution)/shard_map/put_out/pallas_call | solution.py:422
